TPU v7x, 512 devices: a whole 4x4x16 slice. The times are simulated.
512 devices in a mesh: blk: 32 (over x, z_lo), expert: 16 (over z_hi, y, core).
Axes of the slice: x: 4, y: 4, z: 16 (z_hi: 2, z_lo: 8; z = z_hi * 8 + z_lo), core: 2. Of those that a mesh axis runs over, the one named last changes fastest.
Arguments:
- short_draft: bfloat16 [1024, 64, 3, 512], P(('blk', 'expert')), may hold values from -42 to 42
- short_mask: int32 [1024, 64, 64], P(('blk', 'expert')), may hold values from 0 to 1, as said below
- short_keys: bfloat16 [1024, 128, 512], P(('blk', 'expert')), may hold values from -16 to 16
- short_values: bfloat16 [1024, 128, 512], P(('blk', 'expert')), may hold values from -6 to 6
- short_length: int32 [1024], P(('blk', 'expert')), may hold values from 1 to 128, 65536 in all
- short_x: bfloat16 [65536, 1024], P(('blk', 'expert')), may hold values from -44 to 44
- accepted: int32 [1024, 8], P(('blk', 'expert')), may hold values from 0 to 63, as said below
- long_draft: bfloat16 [32, 64, 3, 512], P('expert'), may hold values from -42 to 42
- long_mask: int32 [32, 64, 64], P('expert'), may hold values from 0 to 1, as said below
- long_keys: bfloat16 [32, 8192, 512], P('expert', 'blk'), may hold values from -15 to 15
- long_values: bfloat16 [32, 8192, 512], P('expert', 'blk'), may hold values from -6 to 6
- long_x: bfloat16 [32, 64, 1024], P('expert', 'blk'), may hold values from -44 to 44
- out_weight: bfloat16 [512, 1024], P('expert'), may hold values from -0.25 to 0.25
- norm_gain: bfloat16 [1024], replicated, may hold values from 0.099609375 to 1.8984375
- router: bfloat16 [1024, 16], replicated, may hold values from -0.1875 to 0.1875
- route_ids: int32 [67584, 2], P(('blk', 'expert')), may hold values from 0 to 15, all different within a row; in each aligned block of 132 rows (0 to 131, 132 to 263, ...) at most 21 rows name the same one
- expert_in: bfloat16 [16, 1408, 2, 1024], P('expert', 'blk'), may hold values from -0.1875 to 0.1875
- expert_out: bfloat16 [16, 1408, 1024], P('expert', 'blk'), may hold values from -0.15625 to 0.15625
Outputs:
- short_out: bfloat16 [65536, 1024], P(('blk', 'expert'))
- accepted_out: bfloat16 [1024, 8, 1024], P(('blk', 'expert'))
- long_out: bfloat16 [32, 64, 1024], P('expert', 'blk')
Inputs may be any that keep to these rules, and one draw needn't show every extreme that they name: short_mask[r, i, j] is 1 exactly when tree node j is node i or one of its ancestors; every node but the root 0 has a parent of smaller index. long_mask[r, i, j] is 1 exactly when tree node j is node i or one of its ancestors; every node but the root 0 has a parent of smaller index. accepted[r] lists 8 nodes of request r's tree, the root first and node 63 last, each the parent of the next. `route_ids`: a row's two experts differ; among the rows of one device no expert is named more than 21 times.
All inputs are finite; a program needn't handle non-finite values. No bound on the sum of `short_length` on one device may be relied on, other than what follows from the above.
Results may differ from a plain program's by a relative error of at most 0.011.
Values may be sent and summed in bfloat16 or wider, within the bound.
A program may use at most 64 MiB of HBM per device.

v0:
```python
import jax
import jax.numpy as jnp
from jax import lax
from jax.sharding import PartitionSpec as P

HEADS = 8
HD = 64


def combined_all(part, axis, combine):
    gathered = jax.tree.map(lambda a: lax.all_gather(a, axis), part)

    def take(source):
        return jax.tree.map(lambda a: lax.dynamic_index_in_dim(a, source, 0, False), gathered)

    return lax.fori_loop(
        1, lax.axis_size(axis), lambda source, state: combine(state, take(source)), take(0)
    )


def heads_of(tensor):
    return tensor.reshape(tensor.shape[:-1] + (HEADS, HD))


def block_part(queries, keyside, values, allowed):
    head_size = queries.shape[-1]
    scores = jnp.einsum(
        "rqhe,rkhe->rqhk", queries, keyside, preferred_element_type=jnp.float32
    ) * head_size ** (-0.5)
    scores = jnp.where(allowed[:, :, None, :], scores, -jnp.inf)
    peaks = jnp.max(scores, axis=-1)
    weights = jnp.exp(scores - peaks[..., None]).astype(jnp.bfloat16)
    totals = jnp.sum(weights.astype(jnp.float32), axis=-1)
    output = jnp.einsum("rqhk,rkhe->rqhe", weights, values, preferred_element_type=jnp.float32)
    return (peaks, totals, output.reshape(output.shape[0], output.shape[1], -1))


def expand(factor, output):
    shaped = output.reshape(factor.shape + (-1,))
    return (shaped * factor[..., None]).reshape(output.shape)


def divide(output, totals):
    shaped = output.reshape(totals.shape + (-1,))
    return (shaped / totals[..., None]).reshape(output.shape)


def pair_join(former, latter):
    highest = jnp.maximum(former[0], latter[0])
    former_scale = jnp.exp(former[0] - highest)
    latter_scale = jnp.exp(latter[0] - highest)
    totals = former_scale * former[1] + latter_scale * latter[1]
    output = expand(former_scale, former[2]) + expand(latter_scale, latter[2])
    return (highest, totals, output)


def finish(joined):
    return divide(joined[2], joined[1]).astype(jnp.bfloat16)


def on_device(
    short_draft,
    short_mask,
    short_keys,
    short_values,
    short_length,
    short_x,
    accepted,
    long_draft,
    long_mask,
    long_keys,
    long_values,
    long_x,
    out_weight,
    norm_gain,
    router,
    route_ids,
    expert_in,
    expert_out,
):
    short_count = short_draft.shape[0]
    tree_size = short_draft.shape[1]
    cache_size = short_keys.shape[1]
    model_width = out_weight.shape[1]
    short_queries = heads_of(short_draft[:, :, 0])
    visible = jnp.broadcast_to(
        jnp.arange(cache_size)[None, None, :] < short_length[:, None, None],
        (short_count, tree_size, cache_size),
    )
    short_cache = block_part(short_queries, heads_of(short_keys), heads_of(short_values), visible)
    short_tree = block_part(
        short_queries,
        heads_of(short_draft[:, :, 1]),
        heads_of(short_draft[:, :, 2]),
        short_mask == 1,
    )
    short_attn = finish(pair_join(short_cache, short_tree))
    long_count = long_keys.shape[0]
    cache_local = long_keys.shape[1]
    long_queries = heads_of(long_draft[:, :, 0])
    everything = jnp.ones((long_count, tree_size, cache_local), dtype=bool)
    local_part = block_part(long_queries, heads_of(long_keys), heads_of(long_values), everything)
    share_rows = tree_size // lax.axis_size("blk")
    share_start = lax.axis_index("blk") * share_rows
    merged = combined_all(local_part, "blk", pair_join)
    cache_part = tuple(
        (lax.dynamic_slice_in_dim(member, share_start, share_rows, 1) for member in merged)
    )
    share_queries = lax.dynamic_slice_in_dim(long_queries, share_start, share_rows, 1)
    share_mask = lax.dynamic_slice_in_dim(long_mask, share_start, share_rows, 1)
    long_tree = block_part(
        share_queries, heads_of(long_draft[:, :, 1]), heads_of(long_draft[:, :, 2]), share_mask == 1
    )
    long_attn = finish(pair_join(cache_part, long_tree))
    attn_rows = jnp.concatenate(
        [short_attn.reshape(-1, short_attn.shape[-1]), long_attn.reshape(-1, long_attn.shape[-1])],
        axis=0,
    )
    residual = jnp.concatenate([short_x, long_x.reshape(-1, model_width)], axis=0)
    row_count = attn_rows.shape[0]
    projected = jnp.dot(
        attn_rows,
        lax.all_gather(out_weight, "expert", axis=0, tiled=True),
        preferred_element_type=jnp.float32,
    )
    layer_state = (residual.astype(jnp.float32) + projected).astype(jnp.bfloat16)
    state_wide = layer_state.astype(jnp.float32)
    normed = (
        state_wide
        * lax.rsqrt(jnp.mean(state_wide * state_wide, axis=-1, keepdims=True) + 1e-06)
        * norm_gain.astype(jnp.float32)
    ).astype(jnp.bfloat16)
    gate_probs = jax.nn.sigmoid(jnp.dot(normed, router, preferred_element_type=jnp.float32))
    expert_count = router.shape[1]
    capacity = (row_count * 10 + 4 * expert_count - 1) // (4 * expert_count)
    one_hot = route_ids[:, :, None] == jnp.arange(expert_count, dtype=jnp.int32)[None, None, :]
    gate_pick = jnp.sum(jnp.where(one_hot, gate_probs[:, None, :], 0.0), axis=-1)
    flat_hot = one_hot.reshape(2 * row_count, expert_count).astype(jnp.int32)
    earlier = jnp.cumsum(flat_hot, axis=0) - flat_hot
    slot_in = jnp.sum(earlier * flat_hot, axis=-1)
    target = route_ids.reshape(-1) * capacity + slot_in
    placement = (
        jnp.arange(expert_count * capacity, dtype=jnp.int32)[:, None] == target[None, :]
    ).astype(jnp.bfloat16)
    dispatch = jnp.dot(
        placement, jnp.repeat(normed, 2, axis=0), preferred_element_type=jnp.float32
    ).astype(jnp.bfloat16)
    dispatch = dispatch.reshape(expert_count, capacity, model_width)
    received = lax.all_to_all(dispatch, "expert", split_axis=0, concat_axis=0, tiled=True)
    flat_rows = received.reshape(-1, model_width)
    weight_in = lax.all_gather(expert_in, "blk", axis=1, tiled=True)[0]
    weight_out = lax.all_gather(expert_out, "blk", axis=1, tiled=True)[0]
    gate_part = jnp.einsum(
        "rd,nd->rn", flat_rows, weight_in[:, 0, :], preferred_element_type=jnp.float32
    )
    up_part = jnp.einsum(
        "rd,nd->rn", flat_rows, weight_in[:, 1, :], preferred_element_type=jnp.float32
    )
    inner_act = (jax.nn.gelu(gate_part, approximate=True) * up_part).astype(jnp.bfloat16)
    expert_sum = jnp.dot(inner_act, weight_out, preferred_element_type=jnp.float32)
    expert_y = expert_sum.astype(jnp.bfloat16).reshape(expert_count, capacity, model_width)
    returned = lax.all_to_all(expert_y, "expert", split_axis=0, concat_axis=0, tiled=True)
    per_route = jnp.einsum(
        "sa,sd->ad",
        placement,
        returned.reshape(-1, model_width),
        preferred_element_type=jnp.float32,
    )
    moe_sum = jnp.sum(per_route.reshape(row_count, 2, model_width) * gate_pick[:, :, None], axis=1)
    layer_out = (state_wide + moe_sum).astype(jnp.bfloat16)
    short_total = short_x.shape[0]
    short_out = layer_out[:short_total]
    long_out = layer_out[short_total:].reshape(long_x.shape)
    accepted_out = jnp.take_along_axis(
        short_out.reshape(short_count, tree_size, model_width), accepted[:, :, None], axis=1
    )
    return (short_out, accepted_out, long_out)


def solution(mesh):
    return jax.shard_map(
        on_device,
        mesh=mesh,
        in_specs=(
            P(("blk", "expert"), None, None, None),
            P(("blk", "expert"), None, None),
            P(("blk", "expert"), None, None),
            P(("blk", "expert"), None, None),
            P(("blk", "expert")),
            P(("blk", "expert"), None),
            P(("blk", "expert"), None),
            P("expert", None, None, None),
            P("expert", None, None),
            P("expert", "blk", None),
            P("expert", "blk", None),
            P("expert", "blk", None),
            P("expert", None),
            P(),
            P(),
            P(("blk", "expert"), None),
            P("expert", "blk", None, None),
            P("expert", "blk", None),
        ),
        out_specs=(
            P(("blk", "expert"), None),
            P(("blk", "expert"), None, None),
            P("expert", "blk", None),
        ),
        check_vma=False,
    )
```

profile of v0, /device:TPU:1, one launch (start us, length us, event | category | flops | bytes accessed | tf_op | source)
XLA Modules:
  0.0 905.2 jit_solution(18083236764553195508)
XLA Ops:
  7.2 1.1 fusion.65
  8.5 1.2 copy.132
  14.8 119.0 %all-gather = f32[64,64,8]{1,2,0:T(8,128)S(1)} all-gather(f32[2,64,8]{1,2,0:T(8,128)S(1)} %get-tuple-element.216), channel_id=2, replica_groups=mesh['blk'=32,'expert'=16] {'blk'}, dimensions={0}, use_global_device_ids=true | all-gather | bytes 135168 | tf_op jit(solution)/shard_map/all_gather | solution.py:11
  133.8 103.8 %all-gather.1 = f32[64,64,8]{1,2,0:T(8,128)S(1)} all-gather(f32[2,64,8]{1,2,0:T(8,128)S(1)} %convert_reduce_fusion), channel_id=3, replica_groups=mesh['blk'=32,'expert'=16] {'blk'}, dimensions={0}, use_global_device_ids=true | all-gather | bytes 135168 | tf_op jit(solution)/shard_map/all_gather | solution.py:11
  244.4 9.7 %all-gather.7.cloned.1.call-done = f32[32,2,64,512]{3,2,1,0:T(8,128)} async-done(((f32[1,2,64,512]{3,2,1,0:T(8,128)}), f32[32,2,64,512]{3,2,1,0:T(8,128)}) %all-gather.7.cloned.1.call-update) | async-done | bytes 8388624 | tf_op jit(solution)/shard_map/all_gather | solution.py:11
  255.1 62.8 %while.19 = (s32[]{:T(128)}, f32[2,64,8]{1,2,0:T(8,128)S(1)}, f32[2,64,8]{1,2,0:T(8,128)S(1)}, f32[2,64,512]{2,1,0:T(8,128)S(1)}, f32[32,2,64,8]{2,3,1,0:T(8,128...) while((s32[]{:T(128)}, f32[2,64,8]{1,2,0:T(8,128)S(1)}, ...), condition=%wide.region_7.8_spmd, body=%wide.region_6.7_spmd.sunk | while | flops 202757 | bytes 2941079 | solution.py:16
  258.0 1.1 fusion.84
  260.1 1.1 fusion.84
  262.1 1.1 fusion.84
  272.2 1.1 fusion.84
  274.2 1.1 fusion.84
  290.4 1.1 fusion.84
  318.8 32.4 %all-gather.9.cloned.1.call-done = bf16[512,1024]{1,0:T(8,128)(2,1)} async-done(((bf16[32,1024]{1,0:T(8,128)(2,1)}), bf16[512,1024]{1,0:T(8,128)(2,1)}) %all-gather.9.cloned.1.call-update) | async-done | bytes 1048592 | tf_op jit(solution)/shard_map/all_gather | solution.py:123
  351.2 1.7 multiply_reduce_fusion
  354.1 1.1 reshape.235
  355.2 4.0 all-to-all-start
  359.1 228.4 %all-gather.11.cloned.1.call-done = bf16[1,1408,2,1024]{3,2,0,1:T(2,128)(2,1)} async-done(((bf16[1,44,2,1024]{3,2,0,1:T(2,128)(2,1)}), bf16[1,1408,2,1024]{3,2,0,1:T(2,128)(2,1)}) %all-gather.11.cloned.1.call-update) | async-done | bytes 5767184 | tf_op jit(solution)/shard_map/all_gather | solution.py:151
  587.5 6.9 copy.188
  594.7 4.7 fusion.14
  599.4 228.0 %all-gather.13.cloned.1.call-done = bf16[1,1408,1024]{2,0,1:T(2,128)(2,1)} async-done(((bf16[1,44,1024]{2,0,1:T(2,128)(2,1)}), bf16[1,1408,1024]{2,0,1:T(2,128)(2,1)}) %all-gather.13.cloned.1.call-update) | async-done | bytes 2883600 | tf_op jit(solution)/shard_map/all_gather | solution.py:152
  827.4 6.6 fusion.16
  834.0 1.1 reshape.237
  835.1 33.9 %all-to-all-start.1 = ((bf16[16,21,1024]{2,1,0:T(8,128)(2,1)}), bf16[16,21,1024]{2,1,0:T(8,128)(2,1)S(1)}, u32[]{:S(2)}, u32[]{:S(2)}) async-start(bf16[16,21,1024]{2,1,0:T(8,128)(2,1)} %reshape.237), calls=%async_computation.1 | async-start | bytes 1572864 | tf_op jit(solution)/shard_map/all_to_all | solution.py:162
  869.7 26.1 %all-to-all-done.1 = bf16[16,21,1024]{2,1,0:T(8,128)(2,1)S(1)} async-done(((bf16[16,21,1024]{2,1,0:T(8,128)(2,1)}), bf16[16,21,1024]{2,1,0:T(8,128)(2,1)S(1)}, u32[]{:S(2)}, u32[]{:S(2)}) %all-to-all-start.1) | async-done | bytes 688160 | tf_op jit(solution)/shard_map/all_to_all | solution.py:162
  (359 shorter events, 72.7 us)
Async XLA Ops:
  7.2 862.3 %copy-start = (bf16[1024,16]{0,1:T(8,128)(2,1)S(1)}, bf16[1024,16]{0,1:T(8,128)(2,1)}, u32[]{:S(2)}) copy-start(bf16[1024,16]{0,1:T(8,128)(2,1)} %param.34) | copy-start | bytes 98308
  7.2 2.6 copy-start.2
  7.2 246.9 %all-gather.7.cloned.1.call-start = ((), (), s32[]{:S(2)}) async-start(), calls=%async_computation.2 | async-start | bytes 8650752 | tf_op jit(solution)/shard_map/all_gather | solution.py:11
  10.4 3.1 copy-start.7
  12.0 226.0 %copy-start.3 = (bf16[2,64,3,512]{3,1,2,0:T(8,128)(2,1)S(1)}, bf16[2,64,3,512]{3,1,2,0:T(8,128)(2,1)}, u32[]{:S(2)}) copy-start(bf16[2,64,3,512]{3,1,2,0:T(8,128)(2,1)} %param.20) | copy-start | bytes 1179652
  12.0 339.2 %all-gather.9.cloned.1.call-start = ((), (), s32[]{:S(2)}) async-start(), calls=%async_computation.3 | async-start | bytes 1114112 | tf_op jit(solution)/shard_map/all_gather | solution.py:123
  12.7 574.8 %all-gather.11.cloned.1.call-start = ((), (), s32[]{:S(2)}) async-start(), calls=%async_computation.4 | async-start | bytes 5947392 | tf_op jit(solution)/shard_map/all_gather | solution.py:151
  13.5 813.9 %all-gather.13.cloned.1.call-start = ((), (), s32[]{:S(2)}) async-start(), calls=%async_computation.5 | async-start | bytes 5947392 | tf_op jit(solution)/shard_map/all_gather | solution.py:152
  14.7 223.7 %copy-start.8 = (s32[2,64,64]{2,1,0:T(8,128)S(1)}, s32[2,64,64]{2,1,0:T(8,128)}, u32[]{:S(2)}) copy-start(s32[2,64,64]{2,1,0:T(8,128)} %param.21) | copy-start | bytes 98308
  14.8 223.8 %copy-start.5 = (bf16[2,128,512]{2,1,0:T(8,128)(2,1)S(1)}, bf16[2,128,512]{2,1,0:T(8,128)(2,1)}, u32[]{:S(2)}) copy-start(bf16[2,128,512]{2,1,0:T(8,128)(2,1)} %param.22) | copy-start | bytes 786436
  133.8 105.0 %copy-start.13 = (s32[2]{0:T(128)S(1)}, s32[2]{0:T(128)}, u32[]{:S(2)}) copy-start(s32[2]{0:T(128)} %param.24) | copy-start | bytes 28
  133.8 105.2 %copy-start.6 = (bf16[2,128,512]{2,1,0:T(8,128)(2,1)S(1)}, bf16[2,128,512]{2,1,0:T(8,128)(2,1)}, u32[]{:S(2)}) copy-start(bf16[2,128,512]{2,1,0:T(8,128)(2,1)} %param.23) | copy-start | bytes 786436
  240.7 0.9 copy-start.10
  240.7 0.9 copy-start.11
  240.7 0.9 copy-start.9
  255.1 96.1 %copy-start.4 = (bf16[128,1024]{1,0:T(8,128)(2,1)S(1)}, bf16[128,1024]{1,0:T(8,128)(2,1)}, u32[]{:S(2)}) copy-start(bf16[128,1024]{1,0:T(8,128)(2,1)} %param.25) | copy-start | bytes 786436
  355.2 239.3 %all-to-all-start = ((bf16[16,21,1024]{2,1,0:T(8,128)(2,1)}), bf16[16,21,1024]{2,1,0:T(8,128)(2,1)S(1)}, u32[]{:S(2)}, u32[]{:S(2)}) async-start(bf16[16,21,1024]{2,1,0:T(8,128)(2,1)} %reshape.235), calls=%async_computation | async-start | bytes 1572864 | tf_op jit(solution)/shard_map/all_to_all | solution.py:149
  834.0 35.3 %copy-start.12 = (s32[2,8]{1,0:T(2,128)S(1)}, s32[2,8]{1,0:T(2,128)}, u32[]{:S(2)}) copy-start(s32[2,8]{1,0:T(2,128)} %param.26) | copy-start | bytes 196
  835.1 60.6 %all-to-all-start.1 = ((bf16[16,21,1024]{2,1,0:T(8,128)(2,1)}), bf16[16,21,1024]{2,1,0:T(8,128)(2,1)S(1)}, u32[]{:S(2)}, u32[]{:S(2)}) async-start(bf16[16,21,1024]{2,1,0:T(8,128)(2,1)} %reshape.237), calls=%async_computation.1 | async-start | bytes 1572864 | tf_op jit(solution)/shard_map/all_to_all | solution.py:162
  896.6 2.1 copy-start.1
Sparse Core Ops, SparseCore 0:
  12.1 241.9 all-gather.6
  257.4 93.7 all-gather.8
  353.3 234.1 all-gather.10
  589.4 237.8 all-gather.12
where the time goes:
time: 907 us; the launch traced here: 905 us
  waiting for transfers between devices  526 us (58%)
  blocking collectives  223 us (25%)
  local copies, waits for them, and re-layouts  46.9 us (5%)
  other arithmetic  38.4 us (4%)
  starting transfers between devices  38 us (4%)
  matrix products  16.9 us (2%)
  between operations  14.3 us (2%)
    all_gather x1, waiting for transfers between devices, on_device(): weight_in = lax.all_gather(expert_in, 'blk', axis=1, tiled=True)[0]  228 us
    all_gather x1, waiting for transfers between devices, on_device(): weight_out = lax.all_gather(expert_out, 'blk', axis=1, tiled=True)[0]  228 us
    all_gather x2, blocking collectives, combined_all(): gathered = jax.tree.map(lambda a: lax.all_gather(a, axis), part)  223 us
    all_to_all x1, starting transfers between devices, on_device(): lax.all_to_all(expert_y, 'expert', split_axis=0, concat_axis=0, tiled=True)  33.9 us
    add x31, other arithmetic, pair_join(): output = expand(former_scale, former[2]) + expand(latter_scale, latter[2])  33.7 us
    all_gather x1, waiting for transfers between devices, on_device(): lax.all_gather(out_weight, 'expert', axis=0, tiled=True)  32.4 us
    all_to_all x1, waiting for transfers between devices, on_device(): lax.all_to_all(expert_y, 'expert', split_axis=0, concat_axis=0, tiled=True)  26.1 us
    mul x127, local copies, waits for them, and re-layouts, expand(): return (shaped * factor[..., None]).reshape(output.shape)  21.2 us
  transfers between devices with their start and end apart: 6, of which 5 were waited for; matrix products, arithmetic and copies ran while one was open for 10% of the time, Pallas kernels for 0%

commit v1 on v0

--- a/solution.py
+++ b/solution.py
@@ -149,7 +149,9 @@
     received = lax.all_to_all(dispatch, "expert", split_axis=0, concat_axis=0, tiled=True)
     flat_rows = received.reshape(-1, model_width)
     weight_in = lax.all_gather(expert_in, "blk", axis=1, tiled=True)[0]
-    weight_out = lax.all_gather(expert_out, "blk", axis=1, tiled=True)[0]
+    weight_out = jnp.concatenate(
+        lax.all_to_all(jnp.stack([expert_out] * lax.axis_size("blk")), "blk", 0, 0), axis=1
+    )[0]
     gate_part = jnp.einsum(
         "rd,nd->rn", flat_rows, weight_in[:, 0, :], preferred_element_type=jnp.float32
     )

time: 907 us -> 787 us (0.87)
  waiting for transfers between devices: 526 us -> 178 us
  blocking collectives: 223 us -> 394 us
  starting transfers between devices: 38 us -> 83.7 us
  local copies, waits for them, and re-layouts: 46.9 us -> 57.7 us
    all_gather x1 -> x0, waiting for transfers between devices: 228 us -> none  [on_device(): weight_out = lax.all_gather(expert_out, 'blk', axis=1, tiled=True)[0]]
    all_gather x2, blocking collectives: 223 us -> 394 us  [combined_all(): gathered = jax.tree.map(lambda a: lax.all_gather(a, axis), part)]
    all_gather x1, waiting for transfers between devices: 228 us -> 146 us  [on_device(): weight_in = lax.all_gather(expert_in, 'blk', axis=1, tiled=True)[0]]
    all_to_all x1, starting transfers between devices: 3.98 us -> 39.7 us  [on_device(): lax.all_to_all(dispatch, 'expert', split_axis=0, concat_axis=0, tiled=True)]
    all_gather x1, waiting for transfers between devices: 32.4 us -> 0.02 us  [on_device(): lax.all_gather(out_weight, 'expert', axis=0, tiled=True)]
    all_to_all x0 -> x1, starting transfers between devices: none -> 16 us  [on_device(): lax.all_to_all(jnp.stack([expert_out] * lax.axis_size('blk')), 'blk', 0, 0)]
    all_gather x1, waiting for transfers between devices: 9.65 us -> 0.02 us  [combined_all(): gathered = jax.tree.map(lambda a: lax.all_gather(a, axis), part)]
  transfers between devices with their start and end apart: 6 -> 6, of which waited for: 5 -> 2; matrix products, arithmetic and copies ran while one was open for 10% -> 12% of each run, Pallas kernels for 0% -> 0%
where the time goes in v1:
time: 787 us; the launch traced here: 785 us
  blocking collectives  394 us (50%)
  waiting for transfers between devices  178 us (23%)
  starting transfers between devices  83.7 us (11%)
  local copies, waits for them, and re-layouts  57.7 us (7%)
  other arithmetic  38.4 us (5%)
  matrix products  17.2 us (2%)
  between operations  14.3 us (2%)
    all_gather x2, blocking collectives, combined_all(): gathered = jax.tree.map(lambda a: lax.all_gather(a, axis), part)  394 us
    all_gather x1, waiting for transfers between devices, on_device(): weight_in = lax.all_gather(expert_in, 'blk', axis=1, tiled=True)[0]  146 us
    all_to_all x1, starting transfers between devices, on_device(): lax.all_to_all(dispatch, 'expert', split_axis=0, concat_axis=0, tiled=True)  39.7 us
    add x31, other arithmetic, pair_join(): output = expand(former_scale, former[2]) + expand(latter_scale, latter[2])  33.7 us
    all_to_all x1, waiting for transfers between devices, on_device(): lax.all_to_all(expert_y, 'expert', split_axis=0, concat_axis=0, tiled=True)  30 us
    all_to_all x1, starting transfers between devices, on_device(): lax.all_to_all(expert_y, 'expert', split_axis=0, concat_axis=0, tiled=True)  27.9 us
    mul x127, local copies, waits for them, and re-layouts, expand(): return (shaped * factor[..., None]).reshape(output.shape)  21.2 us
    all_to_all x1, starting transfers between devices, on_device(): lax.all_to_all(jnp.stack([expert_out] * lax.axis_size('blk')), 'blk', 0, 0)  16 us
  transfers between devices with their start and end apart: 6, of which 2 were waited for; matrix products, arithmetic and copies ran while one was open for 12% of the time, Pallas kernels for 0%

profile of v1, /device:TPU:1, one launch (start us, length us, event | category | flops | bytes accessed | tf_op | source)
XLA Modules:
  0.0 785.1 jit_solution(8370357748117925641)
XLA Ops:
  7.2 1.1 fusion.59
  8.5 1.2 copy.101
  12.7 2.0 stack.2
  14.8 16.0 %all-to-all-start.1 = ((bf16[32,1,44,1024]{3,2,1,0:T(8,128)(2,1)}), bf16[32,1,44,1024]{3,2,1,0:T(8,128)(2,1)}, u32[]{:S(2)}, u32[]{:S(2)}) async-start(bf16[32,1,44,1024]{3,2,1,0:T(8,128)(2,1)} %stack.2), calls=%async_computation.1 | async-start | bytes 6291456 | tf_op jit(solution)/shard_map/all_to_all | solution.py:153
  32.0 292.8 %all-gather = f32[64,64,8]{1,2,0:T(8,128)S(1)} all-gather(f32[2,64,8]{1,2,0:T(8,128)S(1)} %get-tuple-element.216), channel_id=2, replica_groups=mesh['blk'=32,'expert'=16] {'blk'}, dimensions={0}, use_global_device_ids=true | all-gather | bytes 135168 | tf_op jit(solution)/shard_map/all_gather | solution.py:11
  325.5 101.3 %all-gather.1 = f32[64,64,8]{1,2,0:T(8,128)S(1)} all-gather(f32[2,64,8]{1,2,0:T(8,128)S(1)} %convert_reduce_fusion), channel_id=3, replica_groups=mesh['blk'=32,'expert'=16] {'blk'}, dimensions={0}, use_global_device_ids=true | all-gather | bytes 135168 | tf_op jit(solution)/shard_map/all_gather | solution.py:11
  428.2 1.1 copy.94
  436.4 62.7 %while.19 = (s32[]{:T(128)}, f32[2,64,8]{1,2,0:T(8,128)S(1)}, f32[2,64,8]{1,2,0:T(8,128)S(1)}, f32[2,64,512]{2,1,0:T(8,128)S(1)}, f32[32,2,64,8]{2,3,1,0:T(8,128...) while((s32[]{:T(128)}, f32[2,64,8]{1,2,0:T(8,128)S(1)}, ...), condition=%wide.region_7.8_spmd, body=%wide.region_6.7_spmd.sunk | while | flops 202757 | bytes 2941079 | solution.py:16
  437.3 1.1 fusion.79
  451.5 1.1 fusion.79
  453.5 1.1 fusion.79
  477.8 1.1 fusion.79
  500.1 1.7 multiply_reduce_fusion
  503.6 1.1 reshape.238
  504.7 39.7 %all-to-all-start = ((bf16[16,21,1024]{2,1,0:T(8,128)(2,1)}), bf16[16,21,1024]{2,1,0:T(8,128)(2,1)S(1)}, u32[]{:S(2)}, u32[]{:S(2)}) async-start(bf16[16,21,1024]{2,1,0:T(8,128)(2,1)} %reshape.238), calls=%async_computation | async-start | bytes 1572864 | tf_op jit(solution)/shard_map/all_to_all | solution.py:149
  544.5 146.4 %all-gather.10.cloned.1.call-done = bf16[1,1408,2,1024]{3,2,0,1:T(2,128)(2,1)} async-done(((bf16[1,44,2,1024]{3,2,0,1:T(2,128)(2,1)}), bf16[1,1408,2,1024]{3,2,0,1:T(2,128)(2,1)}) %all-gather.10.cloned.1.call-update) | async-done | bytes 5767184 | tf_op jit(solution)/shard_map/all_gather | solution.py:151
  690.9 6.9 copy.149
  697.8 5.2 squeeze_reshape.3
  703.0 1.1 reshape.239
  704.1 5.1 fusion.11
  709.2 5.8 convolution_convert_fusion
  715.0 2.2 reshape.240
  717.2 27.9 %all-to-all-start.2 = ((bf16[16,21,1024]{2,1,0:T(8,128)(2,1)}), bf16[16,21,1024]{2,1,0:T(8,128)(2,1)S(1)}, u32[]{:S(2)}, u32[]{:S(2)}) async-start(bf16[16,21,1024]{2,1,0:T(8,128)(2,1)} %reshape.240), calls=%async_computation.2 | async-start | bytes 1572864 | tf_op jit(solution)/shard_map/all_to_all | solution.py:164
  745.7 30.0 %all-to-all-done.2 = bf16[16,21,1024]{2,1,0:T(8,128)(2,1)S(1)} async-done(((bf16[16,21,1024]{2,1,0:T(8,128)(2,1)}), bf16[16,21,1024]{2,1,0:T(8,128)(2,1)S(1)}, u32[]{:S(2)}, u32[]{:S(2)}) %all-to-all-start.2) | async-done | bytes 688160 | tf_op jit(solution)/shard_map/all_to_all | solution.py:164
  (363 shorter events, 75.9 us)
Async XLA Ops:
  7.2 738.3 %copy-start = (bf16[1024,16]{0,1:T(8,128)(2,1)S(1)}, bf16[1024,16]{0,1:T(8,128)(2,1)}, u32[]{:S(2)}) copy-start(bf16[1024,16]{0,1:T(8,128)(2,1)} %param.34) | copy-start | bytes 98308
  7.2 2.6 copy-start.5
  7.2 428.2 %all-gather.6.cloned.1.call-start = ((), (), s32[]{:S(2)}) async-start(), calls=%async_computation.3 | async-start | bytes 8650752 | tf_op jit(solution)/shard_map/all_gather | solution.py:11
  10.4 2.3 copy-start.9
  12.0 488.1 %all-gather.8.cloned.1.call-start = ((), (), s32[]{:S(2)}) async-start(), calls=%async_computation.4 | async-start | bytes 1114112 | tf_op jit(solution)/shard_map/all_gather | solution.py:123
  14.8 490.0 %all-to-all-start.1 = ((bf16[32,1,44,1024]{3,2,1,0:T(8,128)(2,1)}), bf16[32,1,44,1024]{3,2,1,0:T(8,128)(2,1)}, u32[]{:S(2)}, u32[]{:S(2)}) async-start(bf16[32,1,44,1024]{3,2,1,0:T(8,128)(2,1)} %stack.2), calls=%async_computation.1 | async-start | bytes 6291456 | tf_op jit(solution)/shard_map/all_to_all | solution.py:153
  30.8 396.4 %copy-start.6 = (bf16[2,64,3,512]{3,1,2,0:T(8,128)(2,1)S(1)}, bf16[2,64,3,512]{3,1,2,0:T(8,128)(2,1)}, u32[]{:S(2)}) copy-start(bf16[2,64,3,512]{3,1,2,0:T(8,128)(2,1)} %param.20) | copy-start | bytes 1179652
  30.8 660.1 %all-gather.10.cloned.1.call-start = ((), (), s32[]{:S(2)}) async-start(), calls=%async_computation.5 | async-start | bytes 5947392 | tf_op jit(solution)/shard_map/all_gather | solution.py:151
  31.9 395.7 %copy-start.10 = (s32[2,64,64]{2,1,0:T(8,128)S(1)}, s32[2,64,64]{2,1,0:T(8,128)}, u32[]{:S(2)}) copy-start(s32[2,64,64]{2,1,0:T(8,128)} %param.21) | copy-start | bytes 98308
  32.0 395.8 %copy-start.8 = (bf16[2,128,512]{2,1,0:T(8,128)(2,1)S(1)}, bf16[2,128,512]{2,1,0:T(8,128)(2,1)}, u32[]{:S(2)}) copy-start(bf16[2,128,512]{2,1,0:T(8,128)(2,1)} %param.22) | copy-start | bytes 786436
  324.7 103.2 %copy-start.15 = (s32[2]{0:T(128)S(1)}, s32[2]{0:T(128)}, u32[]{:S(2)}) copy-start(s32[2]{0:T(128)} %param.24) | copy-start | bytes 28
  430.9 0.9 copy-start.12
  430.9 0.9 copy-start.13
  430.9 0.9 copy-start.11
  436.4 63.7 %copy-start.7 = (bf16[128,1024]{1,0:T(8,128)(2,1)S(1)}, bf16[128,1024]{1,0:T(8,128)(2,1)}, u32[]{:S(2)}) copy-start(bf16[128,1024]{1,0:T(8,128)(2,1)} %param.25) | copy-start | bytes 786436
  501.9 0.7 copy-start.2
  504.7 198.3 %all-to-all-start = ((bf16[16,21,1024]{2,1,0:T(8,128)(2,1)}), bf16[16,21,1024]{2,1,0:T(8,128)(2,1)S(1)}, u32[]{:S(2)}, u32[]{:S(2)}) async-start(bf16[16,21,1024]{2,1,0:T(8,128)(2,1)} %reshape.238), calls=%async_computation | async-start | bytes 1572864 | tf_op jit(solution)/shard_map/all_to_all | solution.py:149
  704.1 5.1 copy-start.1
  715.0 30.4 %copy-start.14 = (s32[2,8]{1,0:T(2,128)S(1)}, s32[2,8]{1,0:T(2,128)}, u32[]{:S(2)}) copy-start(s32[2,8]{1,0:T(2,128)} %param.26) | copy-start | bytes 196
  715.0 30.5 %copy-start.3 = (bf16[132,1024]{1,0:T(8,128)(2,1)S(1)}, bf16[132,1024]{1,0:T(8,128)(2,1)}, u32[]{:S(2)}) copy-start(bf16[132,1024]{1,0:T(8,128)(2,1)} %copy-done.2) | copy-start | bytes 811012
  717.2 58.5 %all-to-all-start.2 = ((bf16[16,21,1024]{2,1,0:T(8,128)(2,1)}), bf16[16,21,1024]{2,1,0:T(8,128)(2,1)S(1)}, u32[]{:S(2)}, u32[]{:S(2)}) async-start(bf16[16,21,1024]{2,1,0:T(8,128)(2,1)} %reshape.240), calls=%async_computation.2 | async-start | bytes 1572864 | tf_op jit(solution)/shard_map/all_to_all | solution.py:164
  776.5 2.1 copy-start.4
Sparse Core Ops, SparseCore 0:
  12.1 352.3 all-gather.5
  367.8 88.7 all-gather.7
  458.7 232.1 all-gather.9
